TPU v7x, 256 devices: a whole 4x4x8 slice. The times are simulated.
256 devices in a mesh: ia: 32 (over z, x_lo, core), ja: 4 (over y), ka: 2 (over x_hi).
Axes of the slice: x: 4 (x_hi: 2, x_lo: 2; x = x_hi * 2 + x_lo), y: 4, z: 8, core: 2. Of those that a mesh axis runs over, the one named last changes fastest.
Arguments:
- tensor: float32 [8192, 8, 8192], P('ja', 'ka', 'ia'), may hold values from -6 to 6
- factor_a: float32 [8192, 128], P('ia'), may hold values from -1 to 1
- factor_c: float32 [8, 128], P('ka'), may hold values from -2 to 2
- gram_c: float32 [128, 128], replicated, may hold values from -12 to 24, as said below
Outputs:
- factor_b: float32 [8192, 128], P('ja')
- factor_c_new: float32 [8, 128], P('ka')
Inputs may be any that keep to these rules, and one draw needn't show every extreme that they name: `gram_c`: symmetric positive definite.
All inputs are finite; a program needn't handle non-finite values.
Results may differ from a plain program's by a relative error of at most 0.000071.
Values sent between devices are 32-bit elements; how exact they have to be, the bound alone decides.
No kernel may reach another device: no remote copies, remote signals or barrier semaphores. Data moves between devices by JAX's collectives and lax.ppermute only.
A program may use at most 64 MiB of HBM per device.

v0:
```python
import jax
import jax.numpy as jnp
from jax import lax
from jax.sharding import PartitionSpec as P


def right_solve(rhs, system):
    lower = jnp.linalg.cholesky(system)
    middle = lax.linalg.triangular_solve(lower, rhs, left_side=False, lower=True, transpose_a=True)
    return lax.linalg.triangular_solve(
        lower, middle, left_side=False, lower=True, transpose_a=False
    )


def body(tensor, factor_a, factor_c, gram_c):
    high = lax.Precision.HIGHEST
    mode_two, mode_three, mode_one = tensor.shape
    rank = factor_a.shape[1]
    gram_a = lax.psum(
        jnp.dot(factor_a.T, factor_a, precision=high, preferred_element_type=jnp.float32), "ia"
    )
    system_b = gram_a * gram_c
    count = mode_two // lax.axis_size("ia") * lax.axis_size("ia")
    flat = jnp.dot(
        tensor.reshape(count * mode_three, mode_one),
        factor_a,
        precision=high,
        preferred_element_type=jnp.float32,
    )
    shares = lax.psum_scatter(
        flat.reshape(count, mode_three, rank), "ia", scatter_dimension=0, tiled=True
    )
    local_b = lax.psum(jnp.sum(shares * factor_c[None, :, :], axis=1), "ka")
    rows_b = right_solve(local_b, system_b)
    local_c = jnp.sum(shares * rows_b[:, None, :], axis=0)
    local_gram = jnp.dot(rows_b.T, rows_b, precision=high, preferred_element_type=jnp.float32)
    mttkrp_c, gram_b = lax.psum((local_c, local_gram), ("ia", "ja"))
    factor_b = lax.all_gather(rows_b, "ia", axis=0, tiled=True)
    factor_c_new = right_solve(mttkrp_c, gram_a * gram_b)
    return (factor_b, factor_c_new)


def solution(mesh):
    placed = (P("ja", "ka", "ia"), P("ia", None), P("ka", None), P())
    return jax.shard_map(
        body, mesh=mesh, in_specs=placed, out_specs=(P("ja", None), P("ka", None)), check_vma=False
    )
```

profile of v0, /device:TPU:1, one launch (start us, length us, event | category | flops | bytes accessed | tf_op | source)
XLA Modules:
  0.0 1342.1 jit_solution(12914689093623090301)
XLA Ops:
  7.2 0.8 copy-done
  8.1 1.0 fusion.15
  9.2 11.6 fusion
  20.8 0.0 all-reduce.5.cloned.1.call-start
  20.8 0.1 copy.8
  20.9 186.3 %all-reduce.3.cloned.1.call-done = f32[128,128]{0,1:T(8,128)} async-done(((f32[128,128]{0,1:T(8,128)}), f32[128,128]{0,1:T(8,128)}) %all-reduce.3.cloned.1.call-update) | async-done | bytes 65552 | tf_op jit(solution)/shard_map/psum | solution.py:19
  207.2 0.8 mul.24
  208.1 0.1 copy.9
  208.2 11.7 cholesky.44
  220.0 0.6 compare_reduce_fusion.1
  220.6 0.7 fusion.3
  221.3 9.8 custom-call.12
  231.1 97.8 %reduce-scatter.2.cloned.1.call-done = f32[64,4,128]{2,0,1:T(8,128)} async-done(((f32[2048,4,128]{2,0,1:T(8,128)}), f32[64,4,128]{2,0,1:T(8,128)}) %reduce-scatter.2.cloned.1.call-update) | async-done | bytes 131088 | tf_op jit(solution)/shard_map/reduce_scatter | solution.py:30
  328.9 0.9 multiply_reduce_fusion.1
  329.9 9.2 psum.28
  339.0 0.2 fusion.12
  339.2 0.2 fusion.10
  339.5 0.9 fusion.16
  340.5 0.5 all-gather.2.cloned.1.call-update
  341.0 0.9 multiply_reduce_fusion
  341.9 277.2 %psum.30 = f32[4,128]{1,0:T(4,128)S(1)} all-reduce(f32[4,128]{1,0:T(4,128)S(1)} %multiply_reduce_fusion), channel_id=1, replica_groups=mesh['ia'=32,'ja'=4,'ka'=2] {'ia','ja'}, use_global_device_ids=true, to_apply=%region_7.9 | all-reduce | flops 512 | bytes 4096 | tf_op jit(solution)/shard_map/psum | solution.py:37
  619.1 650.4 %all-reduce.5.cloned.1.call-done = f32[128,128]{0,1:T(8,128)} async-done(((f32[128,128]{0,1:T(8,128)}), f32[128,128]{0,1:T(8,128)}) %all-reduce.5.cloned.1.call-update) | async-done | bytes 65552 | tf_op jit(solution)/shard_map/psum | solution.py:37
  1269.6 0.9 mul.27
  1270.4 0.1 copy.11
  1270.6 11.7 cholesky.55
  1282.3 0.6 compare_reduce_fusion
  1282.9 0.7 fusion.4
  1283.6 9.8 custom-call.13
  1293.4 0.2 fusion.7
  1293.6 0.8 fusion.5
  1294.4 38.9 %all-gather.2.cloned.1.call-done = f32[2048,128]{1,0:T(8,128)} async-done(((f32[64,128]{1,0:T(8,128)}), f32[2048,128]{1,0:T(8,128)}) %all-gather.2.cloned.1.call-update) | async-done | bytes 1048592 | tf_op jit(solution)/shard_map/all_gather | solution.py:38
  1333.3 2.3 copy.19
  (17 shorter events, 0.3 us)
Async XLA Ops:
  7.2 0.9 copy-start
  7.2 200.1 %all-reduce.3.cloned.1.call-start = ((), (), s32[]{:S(2)}) async-start(), calls=%async_computation.2 | async-start | bytes 131072 | tf_op jit(solution)/shard_map/psum | solution.py:19
  9.1 11.7 copy-start.2
  9.1 319.8 %copy-start.3 = (f32[4,128]{1,0:T(4,128)S(1)}, f32[4,128]{1,0:T(4,128)}, u32[]{:S(2)}) copy-start(f32[4,128]{1,0:T(4,128)} %param.7) | copy-start | bytes 6148
  9.1 319.8 %reduce-scatter.2.cloned.1.call-start = ((), (), s32[]{:S(2)}) async-start(), calls=%async_computation.1 | async-start | bytes 4325376 | tf_op jit(solution)/shard_map/reduce_scatter | solution.py:30
  20.8 1248.8 %all-reduce.5.cloned.1.call-start = ((), (), s32[]{:S(2)}) async-start(), calls=%async_computation.4 | async-start | bytes 131072 | tf_op jit(solution)/shard_map/psum | solution.py:37
  339.5 1.0 copy-start.1
  340.4 992.9 %all-gather.2.cloned.1.call-start = ((), (), s32[]{:S(2)}) async-start(), calls=%async_computation.3 | async-start | bytes 1081344 | tf_op jit(solution)/shard_map/all_gather | solution.py:38
Sparse Core Ops, SparseCore 0:
  11.2 195.9 all-reduce.2
  209.9 118.9 reduce-scatter.1
  340.5 928.9 all-reduce.4
  1271.3 61.9 all-gather.1
where the time goes:
time: 1340 us
  waiting for transfers between devices  974 us (73%)
  blocking collectives  286 us (21%)
  other arithmetic  49.3 us (4%)
  matrix products  14.9 us (1%)
  between operations  13.9 us (1%)
    psum x1, waiting for transfers between devices, body(): mttkrp_c, gram_b = lax.psum((local_c, local_gram), ('ia', 'ja'))  650 us
    psum x1, blocking collectives, body(): mttkrp_c, gram_b = lax.psum((local_c, local_gram), ('ia', 'ja'))  277 us
    psum x1, waiting for transfers between devices, body(): lax.psum(jnp.dot(factor_a.T, factor_a, precision=high, preferred_element_...  186 us
    reduce_scatter x1, waiting for transfers between devices, body(): lax.psum_scatter(flat.reshape(count, mode_three, rank), 'ia', scatter_dim...  97.8 us
    all_gather x1, waiting for transfers between devices, body(): factor_b = lax.all_gather(rows_b, 'ia', axis=0, tiled=True)  38.9 us
  transfers between devices with their start and end apart: 4, of which 4 were waited for; matrix products, arithmetic and copies ran while one was open for 5% of the time, Pallas kernels for 0%

commit v1 on v0

--- a/solution.py
+++ b/solution.py
@@ -16,8 +16,11 @@
     high = lax.Precision.HIGHEST
     mode_two, mode_three, mode_one = tensor.shape
     rank = factor_a.shape[1]
-    gram_a = lax.psum(
-        jnp.dot(factor_a.T, factor_a, precision=high, preferred_element_type=jnp.float32), "ia"
+    gram_a = jnp.sum(
+        lax.all_gather(
+            jnp.dot(factor_a.T, factor_a, precision=high, preferred_element_type=jnp.float32), "ia"
+        ),
+        axis=0,
     )
     system_b = gram_a * gram_c
     count = mode_two // lax.axis_size("ia") * lax.axis_size("ia")

time: 1340 us -> 1210 us (0.903)
  waiting for transfers between devices: 974 us -> 846 us
    psum x1 -> x0, waiting for transfers between devices: 186 us -> none  [body(): lax.psum(jnp.dot(factor_a.T, factor_a, precision=high, preferred_element_...]
    all_gather x0 -> x1, waiting for transfers between devices: none -> 58.4 us  [body(): lax.all_gather(jnp.dot(factor_a.T, factor_a, precision=high, preferred_el...]
where the time goes in v1:
time: 1210 us
  waiting for transfers between devices  846 us (70%)
  blocking collectives  285 us (24%)
  other arithmetic  50.1 us (4%)
  matrix products  14.9 us (1%)
  between operations  13.9 us (1%)
    psum x1, waiting for transfers between devices, body(): mttkrp_c, gram_b = lax.psum((local_c, local_gram), ('ia', 'ja'))  651 us
    psum x1, blocking collectives, body(): mttkrp_c, gram_b = lax.psum((local_c, local_gram), ('ia', 'ja'))  277 us
    reduce_scatter x1, waiting for transfers between devices, body(): lax.psum_scatter(flat.reshape(count, mode_three, rank), 'ia', scatter_dim...  97.1 us
    all_gather x1, waiting for transfers between devices, body(): lax.all_gather(jnp.dot(factor_a.T, factor_a, precision=high, preferred_el...  58.4 us
    all_gather x1, waiting for transfers between devices, body(): factor_b = lax.all_gather(rows_b, 'ia', axis=0, tiled=True)  39.1 us
    another operation x6, other arithmetic, right_solve(): lower = jnp.linalg.cholesky(system)  24.8 us
  transfers between devices with their start and end apart: 4, of which 4 were waited for; matrix products, arithmetic and copies ran while one was open for 5% of the time, Pallas kernels for 0%

profile of v1, /device:TPU:1, one launch (start us, length us, event | category | flops | bytes accessed | tf_op | source)
XLA Modules:
  0.0 1214.0 jit_solution(15304994901041612694)
XLA Ops:
  7.2 0.8 copy-done
  8.1 1.0 fusion.15
  9.2 11.6 fusion
  20.8 0.1 copy.13
  20.9 58.4 %all-gather.6.cloned.1.call-done = f32[4096,128]{1,0:T(8,128)} async-done(((f32[128,128]{1,0:T(8,128)}), f32[4096,128]{1,0:T(8,128)}) %all-gather.6.cloned.1.call-update) | async-done | bytes 2097168 | tf_op jit(solution)/shard_map/all_gather | solution.py:20
  79.4 1.7 reduce_sum.28
  81.1 0.1 copy.12
  81.2 0.1 copy.14
  81.3 11.7 cholesky.44
  93.0 0.6 compare_reduce_fusion.1
  93.7 0.7 fusion.3
  94.3 9.8 custom-call.12
  104.2 97.1 %reduce-scatter.2.cloned.1.call-done = f32[64,4,128]{2,0,1:T(8,128)} async-done(((f32[2048,4,128]{2,0,1:T(8,128)}), f32[64,4,128]{2,0,1:T(8,128)}) %reduce-scatter.2.cloned.1.call-update) | async-done | bytes 131088 | tf_op jit(solution)/shard_map/reduce_scatter | solution.py:33
  201.2 0.9 multiply_reduce_fusion.1
  202.2 8.6 psum.21
  210.7 0.2 fusion.12
  210.9 0.2 fusion.10
  211.2 0.9 fusion.16
  212.2 0.5 all-gather.4.cloned.1.call-update
  212.7 0.9 multiply_reduce_fusion
  213.6 276.9 %psum.22 = f32[4,128]{1,0:T(4,128)S(1)} all-reduce(f32[4,128]{1,0:T(4,128)S(1)} %multiply_reduce_fusion), channel_id=1, replica_groups=mesh['ia'=32,'ja'=4,'ka'=2] {'ia','ja'}, use_global_device_ids=true, to_apply=%region_7.9 | all-reduce | flops 512 | bytes 4096 | tf_op jit(solution)/shard_map/psum | solution.py:40
  490.5 650.7 %all-reduce.2.cloned.1.call-done = f32[128,128]{0,1:T(8,128)} async-done(((f32[128,128]{0,1:T(8,128)}), f32[128,128]{0,1:T(8,128)}) %all-reduce.2.cloned.1.call-update) | async-done | bytes 65552 | tf_op jit(solution)/shard_map/psum | solution.py:40
  1141.2 0.8 mul.27
  1142.1 0.1 copy.17
  1142.2 11.7 cholesky.55
  1153.9 0.6 compare_reduce_fusion
  1154.6 0.7 fusion.4
  1155.2 9.8 custom-call.13
  1165.0 0.2 fusion.7
  1165.2 0.8 fusion.5
  1166.0 39.1 %all-gather.4.cloned.1.call-done = f32[2048,128]{1,0:T(8,128)} async-done(((f32[64,128]{1,0:T(8,128)}), f32[2048,128]{1,0:T(8,128)}) %all-gather.4.cloned.1.call-update) | async-done | bytes 1048592 | tf_op jit(solution)/shard_map/all_gather | solution.py:41
  1205.2 2.3 copy.23
  (19 shorter events, 0.3 us)
Async XLA Ops:
  7.2 0.9 copy-start
  7.2 72.2 %all-gather.6.cloned.1.call-start = ((), (), s32[]{:S(2)}) async-start(), calls=%async_computation.4 | async-start | bytes 2162688 | tf_op jit(solution)/shard_map/all_gather | solution.py:20
  9.1 11.7 copy-start.2
  9.1 192.1 %copy-start.3 = (f32[4,128]{1,0:T(4,128)S(1)}, f32[4,128]{1,0:T(4,128)}, u32[]{:S(2)}) copy-start(f32[4,128]{1,0:T(4,128)} %param.7) | copy-start | bytes 6148
  9.1 192.1 %reduce-scatter.2.cloned.1.call-start = ((), (), s32[]{:S(2)}) async-start(), calls=%async_computation.1 | async-start | bytes 4325376 | tf_op jit(solution)/shard_map/reduce_scatter | solution.py:33
  20.8 1120.4 %all-reduce.2.cloned.1.call-start = ((), (), s32[]{:S(2)}) async-start(), calls=%async_computation.3 | async-start | bytes 131072 | tf_op jit(solution)/shard_map/psum | solution.py:40
  211.2 1.0 copy-start.1
  212.1 993.0 %all-gather.4.cloned.1.call-start = ((), (), s32[]{:S(2)}) async-start(), calls=%async_computation.2 | async-start | bytes 1081344 | tf_op jit(solution)/shard_map/all_gather | solution.py:41
Sparse Core Ops, SparseCore 0:
  10.4 68.8 all-gather.5
  81.9 119.3 reduce-scatter.1
  212.2 928.9 all-reduce.1
  1143.1 62.0 all-gather.3

commit v2 on v0

--- a/solution.py
+++ b/solution.py
@@ -34,7 +34,7 @@
     rows_b = right_solve(local_b, system_b)
     local_c = jnp.sum(shares * rows_b[:, None, :], axis=0)
     local_gram = jnp.dot(rows_b.T, rows_b, precision=high, preferred_element_type=jnp.float32)
-    mttkrp_c, gram_b = lax.psum((local_c, local_gram), ("ia", "ja"))
+    mttkrp_c, gram_b = lax.psum(lax.psum((local_c, local_gram), "ja"), "ia")
     factor_b = lax.all_gather(rows_b, "ia", axis=0, tiled=True)
     factor_c_new = right_solve(mttkrp_c, gram_a * gram_b)
     return (factor_b, factor_c_new)

time: 1340 us -> 658 us (0.49)
  waiting for transfers between devices: 974 us -> 502 us
  blocking collectives: 286 us -> 74.1 us
    psum x1 -> x2, waiting for transfers between devices: 650 us -> 176 us  [body(): mttkrp_c, gram_b = lax.psum(lax.psum((local_c, local_gram), 'ja'), 'ia')]
    psum x1 -> x2, blocking collectives: 277 us -> 64.9 us  [body(): mttkrp_c, gram_b = lax.psum(lax.psum((local_c, local_gram), 'ja'), 'ia')]
  transfers between devices with their start and end apart: 4 -> 5, of which waited for: 4 -> 5; matrix products, arithmetic and copies ran while one was open for 5% -> 9% of each run, Pallas kernels for 0% -> 0%
where the time goes in v2:
time: 658 us
  waiting for transfers between devices  502 us (76%)
  blocking collectives  74.1 us (11%)
  other arithmetic  49.3 us (7%)
  matrix products  14.9 us (2%)
  between operations  13.9 us (2%)
    psum x1, waiting for transfers between devices, body(): lax.psum(jnp.dot(factor_a.T, factor_a, precision=high, preferred_element_...  186 us
    psum x2, waiting for transfers between devices, body(): mttkrp_c, gram_b = lax.psum(lax.psum((local_c, local_gram), 'ja'), 'ia')  176 us
    reduce_scatter x1, waiting for transfers between devices, body(): lax.psum_scatter(flat.reshape(count, mode_three, rank), 'ia', scatter_dim...  97.8 us
    psum x2, blocking collectives, body(): mttkrp_c, gram_b = lax.psum(lax.psum((local_c, local_gram), 'ja'), 'ia')  64.9 us
    all_gather x1, waiting for transfers between devices, body(): factor_b = lax.all_gather(rows_b, 'ia', axis=0, tiled=True)  40.8 us
    another operation x6, other arithmetic, right_solve(): lower = jnp.linalg.cholesky(system)  24.8 us
    another operation x4, other arithmetic, right_solve(): lax.linalg.triangular_solve(lower, rhs, left_side=False, lower=True, tran...  20.9 us
  transfers between devices with their start and end apart: 5, of which 5 were waited for; matrix products, arithmetic and copies ran while one was open for 9% of the time, Pallas kernels for 0%

profile of v2, /device:TPU:1, one launch (start us, length us, event | category | flops | bytes accessed | tf_op | source)
XLA Modules:
  0.0 657.8 jit_solution(3539378311613307790)
XLA Ops:
  7.2 0.8 copy-done
  8.1 1.0 fusion.15
  9.2 11.6 %fusion = f32[2048,4,128]{2,0,1:T(8,128)} fusion(f32[2048,4,256]{2,1,0:T(4,128)} %param.5, f32[256,128]{1,0:T(8,128)S(1)} %copy-done), kind=kOutput, calls=%fused_computation | convolution fusion | flops 3221225472 | bytes 12713984 | tf_op jit(solution)/shard_map/dot_general | solution.py:24
  20.8 0.1 copy.8
  20.9 186.3 %all-reduce.4.cloned.1.call-done = f32[128,128]{0,1:T(8,128)} async-done(((f32[128,128]{0,1:T(8,128)}), f32[128,128]{0,1:T(8,128)}) %all-reduce.4.cloned.1.call-update) | async-done | bytes 65552 | tf_op jit(solution)/shard_map/psum | solution.py:19
  207.2 0.8 mul.24
  208.2 11.7 %cholesky.44 = f32[128,128]{1,0:T(8,128)S(1)} custom-call(f32[128,128]{1,0:T(8,128)S(1)} %fusion.14), custom_call_target="Cholesky" | custom-call | tf_op jit(solution)/shard_map/jit(cholesky)/cholesky | solution.py:8
  220.0 0.6 compare_reduce_fusion.1
  220.6 0.7 fusion.3
  221.3 9.8 %custom-call.12 = f32[1,128,128]{1,2,0:T(8,128)S(1)} custom-call(f32[1,128,128]{2,1,0:T(8,128)S(1)} %fusion.3), custom_call_target="InvertDiagBlocksLowerTriangular" | custom-call | tf_op jit(solution)/shard_map/triangular_solve | solution.py:9
  231.1 97.8 %reduce-scatter.2.cloned.1.call-done = f32[64,4,128]{2,0,1:T(8,128)} async-done(((f32[2048,4,128]{2,0,1:T(8,128)}), f32[64,4,128]{2,0,1:T(8,128)}) %reduce-scatter.2.cloned.1.call-update) | async-done | bytes 131088 | tf_op jit(solution)/shard_map/reduce_scatter | solution.py:30
  328.9 0.9 multiply_reduce_fusion.1
  329.9 9.2 %psum.42 = f32[64,128]{1,0:T(8,128)S(1)} all-reduce(f32[64,128]{1,0:T(8,128)S(1)} %multiply_reduce_fusion.1), channel_id=1, replica_groups=mesh['ia'=32,'ja'=4,'ka'=2] {'ka'}, use_global_device_ids=true, to_apply=%region_2.0 | all-reduce | flops 8192 | bytes 65536 | tf_op jit(solution)/shard_map/psum | solution.py:33
  339.0 0.2 fusion.12
  339.2 0.2 fusion.10
  339.5 0.9 fusion.16
  340.5 45.8 %all-reduce.6.cloned.1.call-done = f32[128,128]{0,1:T(8,128)} async-done(((f32[128,128]{0,1:T(8,128)}), f32[128,128]{0,1:T(8,128)}) %all-reduce.6.cloned.1.call-update) | async-done | bytes 65552 | tf_op jit(solution)/shard_map/psum | solution.py:37
  386.3 0.5 all-gather.2.cloned.1.call-update
  386.9 0.9 multiply_reduce_fusion
  387.8 7.4 %psum.44 = f32[4,128]{1,0:T(4,128)S(1)} all-reduce(f32[4,128]{1,0:T(4,128)S(1)} %multiply_reduce_fusion), channel_id=1, replica_groups=mesh['ia'=32,'ja'=4,'ka'=2] {'ja'}, use_global_device_ids=true, to_apply=%region_7.0 | all-reduce | flops 512 | bytes 4096 | tf_op jit(solution)/shard_map/psum | solution.py:37
  395.2 57.5 %psum.45 = f32[4,128]{1,0:T(4,128)S(1)} all-reduce(f32[4,128]{1,0:T(4,128)S(1)} %psum.44), channel_id=1, replica_groups=mesh['ia'=32,'ja'=4,'ka'=2] {'ia'}, use_global_device_ids=true, to_apply=%region_8.0 | all-reduce | flops 512 | bytes 4096 | tf_op jit(solution)/shard_map/psum | solution.py:37
  452.7 130.7 %all-reduce.8.cloned.1.call-done = f32[128,128]{0,1:T(8,128)} async-done(((f32[128,128]{0,1:T(8,128)}), f32[128,128]{0,1:T(8,128)}) %all-reduce.8.cloned.1.call-update) | async-done | bytes 65552 | tf_op jit(solution)/shard_map/psum | solution.py:37
  583.4 0.9 mul.27
  584.3 0.1 copy.11
  584.4 11.7 %cholesky.55 = f32[128,128]{1,0:T(8,128)S(1)} custom-call(f32[128,128]{1,0:T(8,128)S(1)} %fusion.9), custom_call_target="Cholesky" | custom-call | tf_op jit(solution)/shard_map/jit(cholesky)/cholesky | solution.py:8
  596.1 0.6 compare_reduce_fusion
  596.8 0.7 fusion.4
  597.4 9.8 %custom-call.13 = f32[1,128,128]{1,2,0:T(8,128)S(1)} custom-call(f32[1,128,128]{2,1,0:T(8,128)S(1)} %fusion.4), custom_call_target="InvertDiagBlocksLowerTriangular" | custom-call | tf_op jit(solution)/shard_map/triangular_solve | solution.py:9
  607.3 0.2 fusion.7
  607.4 0.8 fusion.5
  608.2 40.8 %all-gather.2.cloned.1.call-done = f32[2048,128]{1,0:T(8,128)} async-done(((f32[64,128]{1,0:T(8,128)}), f32[2048,128]{1,0:T(8,128)}) %all-gather.2.cloned.1.call-update) | async-done | bytes 1048592 | tf_op jit(solution)/shard_map/all_gather | solution.py:38
  649.0 2.3 copy.20
  (21 shorter events, 0.5 us)
Async XLA Ops:
  7.2 0.9 copy-start
  7.2 200.1 %all-reduce.4.cloned.1.call-start = ((), (), s32[]{:S(2)}) async-start(), calls=%async_computation.2 | async-start | bytes 131072 | tf_op jit(solution)/shard_map/psum | solution.py:19
  9.1 11.7 %copy-start.2 = (f32[128,128]{1,0:T(8,128)S(1)}, f32[128,128]{1,0:T(8,128)}, u32[]{:S(2)}) copy-start(f32[128,128]{1,0:T(8,128)} %param.8) | copy-start | bytes 196612
  9.1 319.8 %copy-start.3 = (f32[4,128]{1,0:T(4,128)S(1)}, f32[4,128]{1,0:T(4,128)}, u32[]{:S(2)}) copy-start(f32[4,128]{1,0:T(4,128)} %param.7) | copy-start | bytes 6148
  9.1 319.8 %reduce-scatter.2.cloned.1.call-start = ((), (), s32[]{:S(2)}) async-start(), calls=%async_computation.1 | async-start | bytes 4325376 | tf_op jit(solution)/shard_map/reduce_scatter | solution.py:30
  20.8 365.5 %all-reduce.6.cloned.1.call-start = ((), (), s32[]{:S(2)}) async-start(), calls=%async_computation.4 | async-start | bytes 131072 | tf_op jit(solution)/shard_map/psum | solution.py:37
  339.5 46.9 %copy-start.1 = (f32[64,128]{1,0:T(8,128)}, f32[64,128]{1,0:T(8,128)S(1)}, u32[]{:S(2)}) copy-start(f32[64,128]{1,0:T(8,128)S(1)} %fusion.10) | copy-start | bytes 98308
  340.4 243.0 %all-reduce.8.cloned.1.call-start = ((), (), s32[]{:S(2)}) async-start(), calls=%async_computation.5 | async-start | bytes 131072 | tf_op jit(solution)/shard_map/psum | solution.py:37
  386.3 262.7 %all-gather.2.cloned.1.call-start = ((), (), s32[]{:S(2)}) async-start(), calls=%async_computation.3 | async-start | bytes 1081344 | tf_op jit(solution)/shard_map/all_gather | solution.py:38
Sparse Core Ops, SparseCore 0:
  11.2 195.9 all-reduce.3
  209.9 118.9 reduce-scatter.1
  340.5 45.6 all-reduce.5
  388.7 194.6 all-reduce.7
  585.2 63.7 all-gather.1
